TPU v7x, 32 devices: a whole 2x2x4 slice. The times are simulated.
32 devices in a mesh: dp: 8 (over z, y), vocab: 4 (over x, core).
Axes of the slice: x: 2, y: 2, z: 4, core: 2. Of those that a mesh axis runs over, the one named last changes fastest.
Arguments:
- tokens: bfloat16 [1024, 7168], P('dp'), may hold values from -6 to 6
- expert_hidden: bfloat16 [1024, 8, 1024], P('dp'), may hold values from -6 to 6
- routes: int32 [1024, 8], P('dp'), may hold values from 0 to 15, all different within a row; in each aligned block of 32 rows (0 to 31, 32 to 63, ...) at most 24 rows name the same one
- route_weight: float32 [1024, 8], P('dp'), may hold values from 0.05 to 0.45
- expert_weight: bfloat16 [32, 512, 7168], P(('dp', 'vocab')), may hold values from -0.1875 to 0.1875
- norm_gain: float32 [7168], replicated, may hold values from 0.5 to 1.5
- head_weight: bfloat16 [7168, 114688], P(None, ('dp', 'vocab')), may hold values from -8 to 8
- targets: int32 [1024], P('dp'), may hold values from 0 to 114687
- rollout_logprob: float32 [1024], P('dp'), may hold values from -21 to -13
- advantages: float32 [1024], P('dp'), may hold values from -5 to 5
Outputs:
- layer_out: bfloat16 [1024, 7168], P('dp')
- token_logprob: float32 [1024], P('dp')
- token_loss: float32 [1024], P('dp')
Inputs may be any that keep to these rules, and one draw needn't show every extreme that they name: The 8 routes of a token name different experts; among the routes of one aligned block of 32 token rows, no expert is named more than 24 times.
All inputs are finite; a program needn't handle non-finite values.
Results may differ from a plain program's by a relative error of at most 0.02.
Values may be sent and summed in bfloat16 or wider, within the bound.
A program may use at most 192 MiB of HBM per device.

v0:
```python
import jax
import jax.numpy as jnp
from jax import lax
from jax.sharding import PartitionSpec as P

norm_epsilon = 1e-06
clip_low = 0.8
clip_high = 1.2
dual_bound = 3.0


def rms_scale(values, norm_gain):
    widened = values.astype(jnp.float32)
    mean_square = jnp.mean(widened * widened, axis=-1, keepdims=True)
    return (widened * lax.rsqrt(mean_square + norm_epsilon) * norm_gain).astype(jnp.bfloat16)


def clipped_loss(logprob, rollout_logprob, advantages):
    ratio = jnp.exp(logprob - rollout_logprob)
    surrogate = jnp.minimum(ratio * advantages, jnp.clip(ratio, clip_low, clip_high) * advantages)
    bounded = jnp.where(
        advantages < 0.0, jnp.maximum(surrogate, dual_bound * advantages), surrogate
    )
    return -bounded


def per_device(
    tokens,
    expert_hidden,
    routes,
    route_weight,
    expert_weight,
    norm_gain,
    head_weight,
    targets,
    rollout_logprob,
    advantages,
):
    vocab_count = lax.axis_size("vocab")
    device_count = lax.axis_size(("dp", "vocab"))
    experts = device_count // 2
    group_count = tokens.shape[0]
    sub_rows = group_count // vocab_count
    top_count = routes.shape[1]
    capacity = max(2, 3 * sub_rows * top_count // (2 * experts))
    sub_start = lax.axis_index("vocab") * sub_rows
    mine_tokens = lax.dynamic_slice_in_dim(tokens, sub_start, sub_rows, 0)
    mine_hidden = lax.dynamic_slice_in_dim(expert_hidden, sub_start, sub_rows, 0)
    mine_routes = lax.dynamic_slice_in_dim(routes, sub_start, sub_rows, 0)
    mine_weights = lax.dynamic_slice_in_dim(route_weight, sub_start, sub_rows, 0)
    route_list = mine_routes.reshape(-1)
    onehot = (route_list[:, None] == lax.iota(jnp.int32, experts)[None, :]).astype(jnp.int32)
    before = jnp.cumsum(onehot, axis=0) - onehot
    slot_index = jnp.sum(before * onehot, axis=1)
    position = route_list * capacity + slot_index
    select = (lax.iota(jnp.int32, experts * capacity)[:, None] == position[None, :]).astype(
        jnp.bfloat16
    )
    hidden_rows = mine_hidden.reshape(-1, mine_hidden.shape[2])
    half_width = hidden_rows.shape[1] // 2
    lower_buffer = jnp.dot(
        select, hidden_rows[:, :half_width], preferred_element_type=jnp.float32
    ).astype(jnp.bfloat16)
    upper_buffer = jnp.dot(
        select, hidden_rows[:, half_width:], preferred_element_type=jnp.float32
    ).astype(jnp.bfloat16)
    lower_buffer = lower_buffer.reshape(experts, capacity, half_width)
    upper_buffer = upper_buffer.reshape(experts, capacity, half_width)
    buffer = jnp.stack((lower_buffer, upper_buffer), axis=1).reshape(
        device_count, capacity, half_width
    )
    weight_local = expert_weight[0]
    received = lax.all_to_all(buffer, ("dp", "vocab"), split_axis=0, concat_axis=0, tiled=True)
    sources, slot_count, width = received.shape
    product = jnp.dot(
        received.reshape(sources * slot_count, width),
        weight_local,
        preferred_element_type=jnp.float32,
    ).astype(jnp.bfloat16)
    returned = lax.all_to_all(
        product.reshape(sources, slot_count, -1),
        ("dp", "vocab"),
        split_axis=0,
        concat_axis=0,
        tiled=True,
    )
    model_width = returned.shape[2]
    returned = returned.reshape(experts, 2, capacity, model_width)
    lower_back = returned[:, 0].reshape(experts * capacity, model_width)
    upper_back = returned[:, 1].reshape(experts * capacity, model_width)
    contract = (((0,), (0,)), ((), ()))
    route_out = lax.dot_general(select, lower_back, contract, preferred_element_type=jnp.float32)
    route_out = route_out + lax.dot_general(
        select, upper_back, contract, preferred_element_type=jnp.float32
    )
    moe = jnp.sum(
        route_out.reshape(sub_rows, top_count, model_width) * mine_weights[:, :, None], axis=1
    )
    layer_sub = (mine_tokens.astype(jnp.float32) + moe).astype(jnp.bfloat16)
    group_layer = lax.all_gather(layer_sub, "vocab", axis=0, tiled=True)
    voc_dev = head_weight.shape[1]
    column_start = lax.axis_index(("dp", "vocab")) * voc_dev
    normed_sub = rms_scale(layer_sub, norm_gain)
    labels_sub = lax.dynamic_slice_in_dim(targets, sub_start, sub_rows, 0)
    normed = lax.all_gather(normed_sub, ("dp", "vocab"), axis=0, tiled=True)
    labels = lax.all_gather(labels_sub, ("dp", "vocab"), axis=0, tiled=True)
    logits = jnp.dot(normed, head_weight, preferred_element_type=jnp.float32)
    row_peak = jnp.max(logits, axis=1)
    row_total = jnp.sum(jnp.exp(logits - row_peak[:, None]), axis=1)
    columns = column_start + lax.iota(jnp.int32, voc_dev)
    picked = jnp.sum(jnp.where(columns[None, :] == labels[:, None], logits, 0.0), axis=1)
    peak_all = row_peak
    total_all = row_total
    picked_all = picked
    row_stats = (peak_all, total_all, picked_all)
    peak_all, total_all, picked_all = row_stats
    global_peak = lax.pmax(peak_all, ("dp", "vocab"))
    rescaled = total_all * jnp.exp(peak_all - global_peak)
    sum_total, target_logit = lax.psum((rescaled, picked_all), ("dp", "vocab"))
    log_total = global_peak + jnp.log(sum_total)
    logprob_all = target_logit - log_total
    group_start = lax.axis_index("dp") * group_count
    token_logprob = lax.dynamic_slice_in_dim(logprob_all, group_start, group_count, 0)
    token_loss = clipped_loss(token_logprob, rollout_logprob, advantages)
    return (group_layer, token_logprob, token_loss)


def solution(mesh):
    placed = (
        P("dp", None),
        P("dp", None, None),
        P("dp", None),
        P("dp", None),
        P(("dp", "vocab"), None, None),
        P(),
        P(None, ("dp", "vocab")),
        P("dp"),
        P("dp"),
        P("dp"),
    )
    return jax.shard_map(
        per_device,
        mesh=mesh,
        in_specs=placed,
        out_specs=(P("dp", None), P("dp"), P("dp")),
        check_vma=False,
    )
```

profile of v0, /device:TPU:0, one launch (start us, length us, event | category | flops | bytes accessed | tf_op | source)
XLA Modules:
  0.0 602.0 jit_solution(17716764256732814171)
XLA Ops:
  7.2 0.0 copy-start
  7.2 0.9 constant_dynamic-slice_fusion.1
  8.1 0.1 copy.14
  8.2 0.1 eq.53
  8.3 0.1 reshape.68
  8.4 0.6 reduce-window.6
  9.0 0.2 slice_reduce_fusion
  9.2 0.1 fusion.16
  9.3 0.0 copy-done
  9.3 0.3 convolution_convert_fusion.2
  9.6 0.3 convolution_convert_fusion.1
  9.9 0.1 pad_maximum_fusion
  10.0 27.7 %all_to_all.10 = bf16[32,24,512]{2,1,0:T(8,128)(2,1)S(1)} all-to-all(bf16[32,24,512]{2,1,0:T(8,128)(2,1)S(1)} %bitcast.52), channel_id=1, replica_groups=mesh['dp'=8,'vocab'=4] {'dp','vocab'}, dimensions={0} | all-to-all | bytes 1572864 | tf_op jit(solution)/shard_map/all_to_all | solution.py:73
  37.7 11.5 %convolution_convert_fusion = bf16[768,7168]{1,0:T(8,128)(2,1)} fusion(bf16[768,512]{1,0:T(8,128)(2,1)S(1)} %bitcast.55, bf16[1,512,7168]{2,1,0:T(8,128)(2,1)} %param.14), kind=kOutput, calls=%fused_computation.2 | convolution fusion | flops 5642649600 | bytes 19136512 | tf_op jit(solution)/shard_map/dot_general | solution.py:75
  49.2 0.0 copy-start.3
  49.2 3.8 all-to-all-start.1
  53.1 0.0 all-gather.3.cloned.1.call-start
  53.1 0.0 copy-done.3
  53.1 0.1 constant_dynamic-slice_fusion
  53.2 0.1 copy.19
  53.3 243.5 %all-to-all-done.1 = bf16[32,24,7168]{2,1,0:T(8,128)(2,1)} async-done(((bf16[32,24,7168]{2,1,0:T(8,128)(2,1)}), bf16[32,24,7168]{2,1,0:T(8,128)(2,1)}, u32[]{:S(2)}, u32[]{:S(2)}) %all-to-all-start.1) | async-done | bytes 11010080 | tf_op jit(solution)/shard_map/all_to_all | solution.py:80
  296.8 9.0 %fusion.19 = (bf16[16,1,24,7168]{3,2,1,0:T(8,128)(2,1)}, bf16[16,1,24,7168]{3,2,1,0:T(8,128)(2,1)}) fusion(bf16[16,2,24,7168]{3,2,1,0:T(8,128)(2,1)} %bitcast.10), kind=kLoop, calls=%fused_computation.45 | loop fusion | bytes 22020096 | tf_op jit(solution)/shard_map/slice | solution.py:90
  305.8 4.8 fusion.7
  310.6 0.0 slice-done
  310.6 0.0 slice-done.1
  310.7 0.0 copy-start.2
  310.7 0.0 copy-start.4
  310.7 3.9 fusion.3
  314.6 2.0 fusion.4
  316.6 0.0 all-gather.3.cloned.1.call-update
  316.7 0.0 all-gather.5.cloned.1.call-start
  316.7 0.0 copy-done.2
  316.7 2.0 fusion.6
  318.7 0.0 all-gather.5.cloned.1.call-update
  318.8 0.0 copy-done.4
  318.8 0.2 dynamic-slice_dynamic-update-slice_fusion
  319.0 37.7 %all-reduce = s32[1024]{0:T(1024)S(1)} all-reduce(s32[1024]{0:T(1024)S(1)} %dynamic-slice_dynamic-update-slice_fusion), channel_id=1, replica_groups=mesh['dp'=8,'vocab'=4] {'dp','vocab'}, use_global_device_ids=true, to_apply=%add | all-reduce | flops 1024 | bytes 8192
  356.7 0.0 all-gather.3.cloned.1.call-done
  356.7 85.0 %all-gather.5.cloned.1.call-done = bf16[1024,7168]{1,0:T(8,128)(2,1)} async-done(((bf16[32,7168]{1,0:T(8,128)(2,1)}), bf16[1024,7168]{1,0:T(8,128)(2,1)}) %all-gather.5.cloned.1.call-update) | async-done | bytes 14680080 | tf_op jit(solution)/shard_map/all_gather | solution.py:105
  441.7 63.2 %fusion.20 = (f32[1024]{0:T(1024)S(1)}, f32[1024,3584]{1,0:T(8,128)}) fusion(bf16[1024,7168]{1,0:T(8,128)(2,1)} %all-gather.5.cloned.1.call-done, bf16[7168,3584]{1,0:T(8,128)(2,1)} %param.16), kind=kOutput, calls=%fused_computation.46 | convolution fusion | flops 52617019392 | bytes 80744448 | tf_op jit(solution)/shard_map/dot_general | solution.py:107
  505.0 38.6 %pmax.7 = f32[1024]{0:T(1024)S(1)} all-reduce(f32[1024]{0:T(1024)S(1)} %get-tuple-element.13), channel_id=1, replica_groups=mesh['dp'=8,'vocab'=4] {'dp','vocab'}, use_global_device_ids=true, to_apply=%region_8.9 | all-reduce | flops 1024 | bytes 8192 | tf_op jit(solution)/shard_map/pmax | solution.py:117
  543.5 7.6 %exponential_reduce_fusion = (f32[1024]{0:T(1024)S(1)}, f32[1024]{0:T(1024)S(1)}) fusion(f32[1024,3584]{1,0:T(8,128)} %get-tuple-element.14, f32[1024]{0:T(1024)S(1)} %get-tuple-element.13, s32[1024]{0:T(1024)S(1)} %all-reduce, s32[3584]{0:T(1024)S(1)} %iota_add_fusion), kind=kLoop, calls=%fused_computation | loop fusion | flops 18348032 | bytes 14710784 | tf_op jit(solution)/shard_map/reduce_sum | solution.py:109
  551.1 40.6 %all-reduce.1 = (f32[1024]{0:T(1024)S(1)}, f32[1024]{0:T(1024)S(1)}) all-reduce(f32[1024]{0:T(1024)S(1)} %get-tuple-element.4, f32[1024]{0:T(1024)S(1)} %exponential_multiply_fusion), channel_id=1, replica_groups=mesh['dp'=8,'vocab'=4] {'dp','vocab'}, use_global_device_ids=true, to_apply=%region_6.7 | all-reduce | flops 2048 | bytes 16384 | tf_op jit(solution)/shard_map/psum | solution.py:119
  591.7 0.0 copy-done.5
  591.7 0.0 copy-done.6
  591.8 0.6 fusion.18
  592.4 2.8 copy.24
  595.2 0.0 copy-done.1
  (16 shorter events, 0.1 us)
Async XLA Ops:
  7.2 2.1 copy-start
  49.2 3.9 copy-start.3
  49.2 247.5 %all-to-all-start.1 = ((bf16[32,24,7168]{2,1,0:T(8,128)(2,1)}), bf16[32,24,7168]{2,1,0:T(8,128)(2,1)}, u32[]{:S(2)}, u32[]{:S(2)}) async-start(bf16[32,24,7168]{2,1,0:T(8,128)(2,1)} %bitcast.51), calls=%async_computation.1 | async-start | bytes 22020096 | tf_op jit(solution)/shard_map/all_to_all | solution.py:80
  53.1 303.6 %all-gather.3.cloned.1.call-start = ((), (), s32[]{:S(2)}) async-start(), calls=%async_computation.2 | async-start | bytes 2293760 | tf_op jit(solution)/shard_map/all_gather | solution.py:100
  305.8 4.8 slice-start
  305.8 4.8 slice-start.1
  310.7 6.1 %copy-start.2 = (f32[7168]{0:T(1024)S(1)}, f32[7168]{0:T(1024)}, u32[]{:S(2)}) copy-start(f32[7168]{0:T(1024)} %param.15) | copy-start | bytes 86020
  310.7 8.1 %copy-start.4 = (s32[128]{0:T(128)S(1)}, s32[128]{0:T(128)}, u32[]{:S(2)}) copy-start(s32[128]{0:T(128)} %param.17) | copy-start | bytes 1540
  316.7 125.1 %all-gather.5.cloned.1.call-start = ((), (), s32[]{:S(2)}) async-start(), calls=%async_computation.3 | async-start | bytes 15138816 | tf_op jit(solution)/shard_map/all_gather | solution.py:105
  543.5 51.7 %copy-start.1 = (bf16[128,8,1024]{2,1,0:T(8,128)(2,1)S(1)}, bf16[128,8,1024]{2,1,0:T(8,128)(2,1)}, u32[]{:S(2)}) copy-start(bf16[128,8,1024]{2,1,0:T(8,128)(2,1)} %param.11) | copy-start | bytes 6291460
  543.5 48.2 %copy-start.5 = (f32[128]{0:T(128)S(1)}, f32[128]{0:T(128)}, u32[]{:S(2)}) copy-start(f32[128]{0:T(128)} %param.19) | copy-start | bytes 1540
  543.5 48.2 %copy-start.6 = (f32[128]{0:T(128)S(1)}, f32[128]{0:T(128)}, u32[]{:S(2)}) copy-start(f32[128]{0:T(128)} %param.18) | copy-start | bytes 1540
Sparse Core Ops, SparseCore 0:
  316.8 17.6 all-gather.2
  337.3 104.3 all-gather.4
where the time goes:
time: 603 us; the launch traced here: 602 us
  waiting for transfers between devices  329 us (55%)
  blocking collectives  145 us (24%)
  matrix products  84 us (14%)
  between operations  14.2 us (2%)
  local copies, waits for them, and re-layouts  13.7 us (2%)
  other arithmetic  13 us (2%)
    all_to_all x1, waiting for transfers between devices, per_device(): lax.all_to_all(product.reshape(sources, slot_count, -1), ('dp', 'vocab'),...  243 us
    all_gather x1, waiting for transfers between devices, per_device(): normed = lax.all_gather(normed_sub, ('dp', 'vocab'), axis=0, tiled=True)  85 us
    dot_general x1, matrix products, per_device(): logits = jnp.dot(normed, head_weight, preferred_element_type=jnp.float32)  63.2 us
    psum x1, blocking collectives, per_device(): sum_total, target_logit = lax.psum((rescaled, picked_all), ('dp', 'vocab'))  40.6 us
    pmax x1, blocking collectives, per_device(): global_peak = lax.pmax(peak_all, ('dp', 'vocab'))  38.6 us
    unnamed x1, blocking collectives  37.7 us
    all_to_all x1, blocking collectives, per_device(): lax.all_to_all(buffer, ('dp', 'vocab'), split_axis=0, concat_axis=0, tile...  27.7 us
  transfers between devices with their start and end apart: 3, of which 2 were waited for; matrix products, arithmetic and copies ran while one was open for 0% of the time, Pallas kernels for 0%

commit v1 on v0

v1 whole, which is shorter than its diff:
```python
import functools

import jax
import jax.numpy as jnp
from jax import lax
from jax.experimental import pallas as pl
from jax.experimental.pallas import tpu as pltpu
from jax.sharding import PartitionSpec as P

norm_epsilon = 1e-06
clip_low = 0.8
clip_high = 1.2
dual_bound = 3.0
MESH = pl.DeviceIdType.MESH


def clipped_loss(logprob, rollout_logprob, advantages):
    ratio = jnp.exp(logprob - rollout_logprob)
    surrogate = jnp.minimum(ratio * advantages, jnp.clip(ratio, clip_low, clip_high) * advantages)
    bounded = jnp.where(
        advantages < 0.0, jnp.maximum(surrogate, dual_bound * advantages), surrogate
    )
    return -bounded


def own_position(vocab_count):
    return lax.axis_index("dp") * vocab_count + lax.axis_index("vocab")


def exchange_kernel(count, vocab_count, kinds, *refs):
    number = len(kinds)
    ins, outs = refs[:number], refs[number : 2 * number]
    send_sem, recv_sem, local_sem = refs[2 * number :]
    me = own_position(vocab_count)
    barrier = pltpu.get_barrier_semaphore()

    def place(index):
        return (index // vocab_count, index % vocab_count)

    def source(which, target):
        if kinds[which] == "all":
            return ins[which]
        if kinds[which] == "group":
            return ins[which].at[target // vocab_count]
        return ins[which].at[target]

    def greet(step, carry):
        pl.semaphore_signal(
            barrier, inc=1, device_id=place((me + step) % count), device_id_type=MESH
        )
        return carry

    lax.fori_loop(1, count, greet, 0)
    pl.semaphore_wait(barrier, count - 1)

    def copy(which, target, sender):
        return pltpu.make_async_remote_copy(
            src_ref=source(which, target),
            dst_ref=outs[which].at[sender],
            send_sem=send_sem.at[which, target],
            recv_sem=recv_sem.at[which, sender],
            device_id=place(target),
            device_id_type=MESH,
        )

    def send(step, carry):
        target = (me + step) % count
        for which in range(number):
            copy(which, target, me).start()
        return carry

    lax.fori_loop(1, count, send, 0)
    for which in range(number):
        pltpu.make_async_copy(source(which, me), outs[which].at[me], local_sem.at[which]).start()

    def finish(step, carry):
        target = (me + step) % count
        sender = (me + count - step) % count
        for which in range(number):
            copy(which, target, me).wait_send()
            copy(which, target, sender).wait_recv()
        return carry

    lax.fori_loop(1, count, finish, 0)
    for which in range(number):
        pltpu.make_async_copy(source(which, me), outs[which].at[me], local_sem.at[which]).wait()


def exchange(arrays, kinds, count, vocab_count, identity):
    shapes = []
    for array, kind in zip(arrays, kinds):
        tail = array.shape if kind == "all" else array.shape[1:]
        shapes.append(jax.ShapeDtypeStruct((count,) + tail, array.dtype))
    number = len(arrays)
    return pl.pallas_call(
        functools.partial(exchange_kernel, count, vocab_count, kinds),
        out_shape=shapes,
        in_specs=[pl.BlockSpec(memory_space=pltpu.VMEM)] * number,
        out_specs=[pl.BlockSpec(memory_space=pltpu.VMEM)] * number,
        scratch_shapes=[
            pltpu.SemaphoreType.DMA((number, count)),
            pltpu.SemaphoreType.DMA((number, count)),
            pltpu.SemaphoreType.DMA((number,)),
        ],
        compiler_params=pltpu.CompilerParams(
            collective_id=identity, has_side_effects=True, vmem_limit_bytes=16 * 2**20
        ),
    )(*arrays)


def combine_kernel(
    bit_count,
    vocab_count,
    orders,
    cuts,
    part_ref,
    token_ref,
    gain_ref,
    layer,
    normed,
    held,
    *rest,
):
    slots = rest[:bit_count]
    send_sem, recv_sem, load_sem = rest[bit_count:]
    chains = len(orders)
    me = own_position(vocab_count)
    bits = [(me // (1 << b)) % 2 for b in range(bit_count)]

    def partner(b):
        other = me + (1 - 2 * bits[b]) * (1 << b)
        return (other // vocab_count, other % vocab_count)

    barrier = pltpu.get_barrier_semaphore()
    friends = [partner(b) for b in range(bit_count)]
    for friend in friends:
        pl.semaphore_signal(barrier, inc=1, device_id=friend, device_id_type=MESH)
    pl.semaphore_wait(barrier, len(friends))

    def index(chosen, low):
        return tuple(
            chosen[b] if b in chosen else slice(None) for b in range(bit_count - 1, low - 1, -1)
        )

    def span(chain):
        return pl.ds(cuts[chain], cuts[chain + 1] - cuts[chain])

    def load(chain):
        where = index({0: bits[0]}, 0) + (slice(None), span(chain))
        return pltpu.make_async_copy(
            part_ref.at[where],
            held.at[index({}, 1) + (slice(None), span(chain))],
            load_sem.at[chain],
        )

    def scatter(chain, stage):
        b = orders[chain][stage]
        if stage == 0:
            src = part_ref.at[index({0: 1 - bits[0]}, 0) + (slice(None), span(chain))]
        else:
            chosen = {f: bits[f] for f in orders[chain][1:stage]}
            chosen[b] = 1 - bits[b]
            src = held.at[index(chosen, 1) + (slice(None), span(chain))]
        free = bit_count - 1 - stage
        dst = slots[stage].at[(slice(None),) * (free + 1) + (span(chain),)]
        return pltpu.make_async_remote_copy(
            src_ref=src,
            dst_ref=dst,
            send_sem=send_sem.at[chain, stage],
            recv_sem=recv_sem.at[chain, stage],
            device_id=partner(b),
            device_id_type=MESH,
        )

    def add(chain, stage):
        order = orders[chain]
        fixed = order[1 : stage + 1]
        free = [f for f in range(bit_count - 1, 0, -1) if f not in fixed]
        blocks = 1 << len(free)

        def body(j, carry):
            values = {f: (j // (1 << q)) % 2 for q, f in enumerate(reversed(free))}
            at_slot = tuple(values[f] for f in free) + (slice(None), span(chain))
            values.update({f: bits[f] for f in fixed})
            at_held = index(values, 1) + (slice(None), span(chain))
            held[at_held] = (
                held[at_held].astype(jnp.float32) + slots[stage][at_slot].astype(jnp.float32)
            ).astype(jnp.bfloat16)
            return carry

        if stage < bit_count - 1:
            lax.fori_loop(0, blocks, body, 0)
        else:
            at_held = index({f: bits[f] for f in fixed}, 1) + (slice(None), span(chain))
            total = held[at_held].astype(jnp.float32)
            total = total + slots[stage][slice(None), span(chain)].astype(jnp.float32)
            total = total + token_ref[:, span(chain)].astype(jnp.float32)
            layer[:, span(chain)] = total.astype(jnp.bfloat16)

    for chain in range(chains):
        scatter(chain, 0).start()
    for chain in range(chains):
        load(chain).start()
    for stage in range(bit_count):
        for chain in range(chains):
            if stage == 0:
                load(chain).wait()
            scatter(chain, stage).wait_recv()
            add(chain, stage)
            if stage + 1 < bit_count:
                scatter(chain, stage + 1).start()

    rows = layer[...].astype(jnp.float32)
    mean_square = jnp.mean(rows * rows, axis=-1, keepdims=True)
    normed[...] = (rows * lax.rsqrt(mean_square + norm_epsilon) * gain_ref[...]).astype(
        jnp.bfloat16
    )
    for chain in range(chains):
        for stage in range(bit_count):
            scatter(chain, stage).wait_send()


def head_kernel(
    bit_count,
    vocab_count,
    orders,
    cuts,
    tile,
    normed_ref,
    layer_ref,
    label_ref,
    head_ref,
    stats_ref,
    group_ref,
    rows_all,
    logits,
    weights,
    ici_send,
    ici_recv,
    core_send,
    core_recv,
    weight_sem,
    own_sem,
    group_send,
    group_recv,
):
    chains = len(orders)
    me = own_position(vocab_count)
    my_vocab = lax.axis_index("vocab")
    bits = [(me // (1 << b)) % 2 for b in range(bit_count)]
    vocab_bits = vocab_count.bit_length() - 1
    columns = head_ref.shape[1]
    tiles = columns // tile
    stages = bit_count - 1
    widths = [cuts[c + 1] - cuts[c] for c in range(chains)]

    def partner(b):
        other = me + (1 - 2 * bits[b]) * (1 << b)
        return (other // vocab_count, other % vocab_count)

    def index(chosen):
        return tuple(
            chosen[b] if b in chosen else slice(None) for b in range(bit_count - 1, -1, -1)
        )

    def span(chain):
        return pl.ds(cuts[chain], widths[chain])

    turns = [(chain, 0) for chain in range(chains)] + [(chain, 1) for chain in range(chains)]

    def fetch(turn, column, slot):
        chain = turns[turn][0]
        return pltpu.make_async_copy(
            head_ref.at[span(chain), pl.ds(pl.multiple_of(column * tile, tile), tile)],
            weights.at[slot, pl.ds(0, widths[chain])],
            weight_sem.at[slot],
        )

    fetch(0, 0, 0).start()
    fetch(0, 1, 1).start()

    barrier = pltpu.get_barrier_semaphore()
    for b in range(bit_count):
        pl.semaphore_signal(barrier, inc=1, device_id=partner(b), device_id_type=MESH)
    pl.semaphore_wait(barrier, bit_count)

    own = pltpu.make_async_copy(
        normed_ref, rows_all.at[index({b: bits[b] for b in range(bit_count)})], own_sem.at[0]
    )
    own.start()
    own_group = pltpu.make_async_copy(layer_ref, group_ref.at[my_vocab], own_sem.at[1])
    own_group.start()
    own.wait()

    def remote(where, sends, recvs, b):
        return pltpu.make_async_remote_copy(
            src_ref=rows_all.at[where],
            dst_ref=rows_all.at[where],
            send_sem=sends,
            recv_sem=recvs,
            device_id=partner(b),
            device_id_type=MESH,
        )

    def spread(chain, stage):
        order = orders[chain]
        where = index({f: bits[f] for f in order[: bit_count - stage]}) + (slice(None), span(chain))
        return remote(
            where,
            ici_send.at[chain, stage],
            ici_recv.at[chain, stage],
            order[bit_count - 1 - stage],
        )

    def side(chain, half):
        bit = bits[orders[chain][1]]
        return bit if half == 0 else 1 - bit

    def across(chain, half):
        where = index({0: bits[0], orders[chain][1]: side(chain, half)}) + (
            slice(None),
            span(chain),
        )
        return remote(where, core_send.at[chain, half], core_recv.at[chain, half], 0)

    def group(b):
        held_count = vocab_count >> (b + 1)
        step = 1 << (b + 1)
        copies = []
        for q in range(held_count):
            position = q * step + my_vocab % step
            copies.append(
                pltpu.make_async_remote_copy(
                    src_ref=group_ref.at[position],
                    dst_ref=group_ref.at[position],
                    send_sem=group_send.at[b, q],
                    recv_sem=group_recv.at[b, q],
                    device_id=partner(b),
                    device_id_type=MESH,
                )
            )
        return copies

    for chain in range(chains):
        spread(chain, 0).start()

    def clear(j, carry):
        at = tuple((j // (1 << b)) % 2 for b in range(bit_count - 1, -1, -1))
        logits[at] = jnp.zeros(logits.shape[bit_count:], jnp.float32)
        return carry

    lax.fori_loop(0, 1 << bit_count, clear, 0)
    for stage in range(stages - 1):
        for chain in range(chains):
            spread(chain, stage).wait_recv()
            spread(chain, stage + 1).start()
            if stage == stages - 2:
                across(chain, 0).start()
    own_group.wait()

    count = len(turns)
    for turn in range(count):
        chain, half = turns[turn]
        if half == 0:
            across(chain, 0).wait_recv()
        else:
            if chain == 0:
                for other in range(chains):
                    spread(other, stages - 1).wait_recv()
                    across(other, 1).start()
                for copy in group(vocab_bits - 1):
                    copy.start()
            across(chain, 1).wait_recv()
            if chain > 0:
                b = vocab_bits - 1 - chain
                if b >= 0:
                    for copy in group(b + 1):
                        copy.wait_recv()
                    for copy in group(b):
                        copy.start()
        fixed = orders[chain][1]
        where = index({fixed: side(chain, half)})

        def body(column, carry):
            slot = (turn * tiles + column) % 3
            fetch(turn, column, slot).wait()

            @pl.when(column + 2 < tiles)
            def _():
                fetch(turn, column + 2, (turn * tiles + column + 2) % 3).start()

            if turn + 1 < count:

                @pl.when(column + 2 >= tiles)
                def _():
                    fetch(
                        turn + 1, column + 2 - tiles, (turn * tiles + column + 2) % 3
                    ).start()

            left = rows_all[where + (slice(None), span(chain))]
            shape = left.shape[:-1]
            left = left.reshape(-1, widths[chain])
            product = jnp.dot(
                left, weights[slot, : widths[chain]], preferred_element_type=jnp.float32
            ).reshape(shape + (tile,))
            at = where + (slice(None), pl.ds(pl.multiple_of(column * tile, tile), tile))
            logits[at] += product
            return carry

        lax.fori_loop(0, tiles, body, 0)

    waited = vocab_bits - 1 - (chains - 1)
    for b in range(max(waited, 0), -1, -1):
        for copy in group(b):
            if b < waited:
                copy.start()
            copy.wait_recv()

    first_column = me * columns
    lanes = lax.broadcasted_iota(jnp.int32, (1, columns), 1) + first_column
    stat_lane = lax.broadcasted_iota(jnp.int32, (1, 128), 1)

    def reduce_block(j, carry):
        at = tuple((j // (1 << b)) % 2 for b in range(bit_count - 1, -1, -1))
        values = logits[at]
        peak = jnp.max(values, axis=1, keepdims=True)
        total = jnp.sum(jnp.exp(values - peak), axis=1, keepdims=True)
        match = lanes == label_ref[j]
        picked = jnp.sum(jnp.where(match, values, 0.0), axis=1, keepdims=True)
        stats_ref[j] = jnp.where(
            stat_lane == 0, peak, jnp.where(stat_lane == 1, total, picked)
        )
        return carry

    lax.fori_loop(0, 1 << bit_count, reduce_block, 0)

    for chain in range(chains):
        for stage in range(stages):
            spread(chain, stage).wait_send()
        across(chain, 0).wait_send()
        across(chain, 1).wait_send()
    for b in range(vocab_bits):
        for copy in group(b):
            copy.wait_send()


def axis_plan(device_count, vocab_count, width):
    bit_count = device_count.bit_length() - 1
    vocab_bits = vocab_count.bit_length() - 1
    low = vocab_bits + (bit_count - vocab_bits) // 2
    first = list(range(1, vocab_bits))
    second = list(range(vocab_bits, low))
    third = list(range(low, bit_count))
    orders = [[0] + first + second + third, [0] + second + first + third, [0] + third + first + second]
    lanes = width // 128
    cuts = [0, 128 * (lanes // 3), 128 * (2 * lanes // 3), width]
    return bit_count, orders, cuts


def combine(part, tokens, gain, device_count, vocab_count):
    rows, width = tokens.shape
    bit_count, orders, cuts = axis_plan(device_count, vocab_count, width)
    part = part.reshape((2,) * bit_count + (rows, width))
    scratch = [pltpu.VMEM((2,) * (bit_count - 1) + (rows, width), jnp.bfloat16)]
    for stage in range(bit_count):
        scratch.append(pltpu.VMEM((2,) * (bit_count - 1 - stage) + (rows, width), jnp.bfloat16))
    chains = len(orders)
    scratch += [pltpu.SemaphoreType.DMA((chains, bit_count))] * 2
    scratch += [pltpu.SemaphoreType.DMA((chains,))]
    return pl.pallas_call(
        functools.partial(combine_kernel, bit_count, vocab_count, orders, cuts),
        out_shape=[jax.ShapeDtypeStruct((rows, width), jnp.bfloat16)] * 2,
        in_specs=[
            pl.BlockSpec(memory_space=pl.ANY),
            pl.BlockSpec(memory_space=pltpu.VMEM),
            pl.BlockSpec(memory_space=pltpu.VMEM),
        ],
        out_specs=[pl.BlockSpec(memory_space=pltpu.VMEM)] * 2,
        scratch_shapes=scratch,
        compiler_params=pltpu.CompilerParams(
            collective_id=1, has_side_effects=True, vmem_limit_bytes=58 * 2**20
        ),
    )(part, tokens, gain)


def head(normed, layer, labels, head_weight, device_count, vocab_count):
    rows, width = normed.shape
    columns = head_weight.shape[1]
    tile = 512 if columns % 512 == 0 else 128
    bit_count, orders, cuts = axis_plan(device_count, vocab_count, width)
    chains = len(orders)
    vocab_bits = vocab_count.bit_length() - 1
    widest = max(cuts[c + 1] - cuts[c] for c in range(chains))
    lead = (2,) * bit_count
    stats, group = pl.pallas_call(
        functools.partial(head_kernel, bit_count, vocab_count, orders, cuts, tile),
        out_shape=[
            jax.ShapeDtypeStruct((device_count, rows, 128), jnp.float32),
            jax.ShapeDtypeStruct((vocab_count, rows, width), jnp.bfloat16),
        ],
        in_specs=[
            pl.BlockSpec(memory_space=pltpu.VMEM),
            pl.BlockSpec(memory_space=pltpu.VMEM),
            pl.BlockSpec(memory_space=pltpu.VMEM),
            pl.BlockSpec(memory_space=pl.ANY),
        ],
        out_specs=[
            pl.BlockSpec(memory_space=pltpu.VMEM),
            pl.BlockSpec(memory_space=pl.ANY),
        ],
        scratch_shapes=[
            pltpu.VMEM(lead + (rows, width), jnp.bfloat16),
            pltpu.VMEM(lead + (rows, columns), jnp.float32),
            pltpu.VMEM((3, widest, tile), jnp.bfloat16),
            pltpu.SemaphoreType.DMA((chains, bit_count - 1)),
            pltpu.SemaphoreType.DMA((chains, bit_count - 1)),
            pltpu.SemaphoreType.DMA((chains, 2)),
            pltpu.SemaphoreType.DMA((chains, 2)),
            pltpu.SemaphoreType.DMA((3,)),
            pltpu.SemaphoreType.DMA((2,)),
            pltpu.SemaphoreType.DMA((vocab_bits, vocab_count // 2)),
            pltpu.SemaphoreType.DMA((vocab_bits, vocab_count // 2)),
        ],
        compiler_params=pltpu.CompilerParams(
            collective_id=3, has_side_effects=True, vmem_limit_bytes=60 * 2**20
        ),
    )(normed, layer, labels, head_weight)
    return stats, group.reshape(vocab_count * rows, width)


def per_device(
    tokens,
    expert_hidden,
    routes,
    route_weight,
    expert_weight,
    norm_gain,
    head_weight,
    targets,
    rollout_logprob,
    advantages,
):
    vocab_count = lax.axis_size("vocab")
    device_count = lax.axis_size(("dp", "vocab"))
    experts = device_count // 2
    group_count = tokens.shape[0]
    sub_rows = group_count // vocab_count
    top_count = routes.shape[1]
    sub_start = lax.axis_index("vocab") * sub_rows
    mine_tokens = lax.dynamic_slice_in_dim(tokens, sub_start, sub_rows, 0)
    mine_hidden = lax.dynamic_slice_in_dim(expert_hidden, sub_start, sub_rows, 0)
    mine_routes = lax.dynamic_slice_in_dim(routes, sub_start, sub_rows, 0)
    mine_weights = lax.dynamic_slice_in_dim(route_weight, sub_start, sub_rows, 0)
    labels_sub = lax.dynamic_slice_in_dim(targets, sub_start, sub_rows, 0)
    hidden_rows = mine_hidden.reshape(-1, mine_hidden.shape[2])
    half_width = hidden_rows.shape[1] // 2
    route_list = mine_routes.reshape(-1)
    weight_list = mine_weights.reshape(-1)
    named = jnp.where(
        lax.iota(jnp.int32, experts)[:, None] == route_list[None, :], weight_list[None, :], 0.0
    )
    row_of = lax.iota(jnp.int32, sub_rows * top_count) // top_count
    same_row = lax.iota(jnp.int32, sub_rows)[:, None] == row_of[None, :]
    select = jnp.where(same_row[None], named[:, None], 0.0).astype(jnp.bfloat16)
    select = select.reshape(experts * sub_rows, sub_rows * top_count)
    dense = jnp.dot(select, hidden_rows, preferred_element_type=jnp.float32).astype(jnp.bfloat16)
    dense = dense.reshape(experts, sub_rows, 2, half_width).transpose(0, 2, 1, 3)
    dense = dense.reshape(device_count, sub_rows, half_width)
    label_tile = jnp.broadcast_to(
        jnp.pad(labels_sub, (0, 128 - sub_rows))[None, :], (8, 128)
    )
    received, label_tiles = exchange(
        [dense, label_tile], ("each", "all"), device_count, vocab_count, 0
    )
    labels = label_tiles[:, 0, :sub_rows].reshape(-1)
    part = jnp.dot(
        received.reshape(device_count * sub_rows, half_width),
        expert_weight[0],
        preferred_element_type=jnp.float32,
    ).astype(jnp.bfloat16)
    layer_sub, normed = combine(
        part, mine_tokens, norm_gain[None, :], device_count, vocab_count
    )
    labels = labels.reshape(device_count, sub_rows, 1)
    stats_rows, group_layer = head(
        normed, layer_sub, labels, head_weight, device_count, vocab_count
    )
    stats = stats_rows[:, :, :8].reshape(-1, group_count, 8).transpose(0, 2, 1)
    (stats_all,) = exchange([stats], ("group",), device_count, vocab_count, 2)
    peaks, totals, picks = stats_all[:, 0], stats_all[:, 1], stats_all[:, 2]
    peak = jnp.max(peaks, axis=0)
    total = jnp.sum(totals * jnp.exp(peaks - peak[None]), axis=0)
    token_logprob = jnp.sum(picks, axis=0) - (peak + jnp.log(total))
    token_loss = clipped_loss(token_logprob, rollout_logprob, advantages)
    return (group_layer, token_logprob, token_loss)


def solution(mesh):
    placed = (
        P("dp", None),
        P("dp", None, None),
        P("dp", None),
        P("dp", None),
        P(("dp", "vocab"), None, None),
        P(),
        P(None, ("dp", "vocab")),
        P("dp"),
        P("dp"),
        P("dp"),
    )
    return jax.shard_map(
        per_device,
        mesh=mesh,
        in_specs=placed,
        out_specs=(P("dp", None), P("dp"), P("dp")),
        check_vma=False,
    )
```

time: 603 us -> 297 us (0.49)
  waiting for transfers between devices: 329 us -> 0 us
  Pallas kernels: 0 us -> 270 us
  blocking collectives: 145 us -> 0 us
  matrix products: 84 us -> 14.7 us
  between operations: 14.2 us -> 0.76 us
  other arithmetic: 13 us -> 0.7 us
    pallas_call x0 -> x4, Pallas kernels: none -> 270 us  [the longest x1 128 us: head(): pl.pallas_call(functools.partial(head_kernel, bit_count, vocab_count, ord...]
    all_to_all x1 -> x0, waiting for transfers between devices: 243 us -> none  [per_device(): lax.all_to_all(product.reshape(sources, slot_count, -1), ('dp', 'vocab'),...]
    all_gather x2 -> x0, waiting for transfers between devices: 85 us -> none  [the longest x1 85 us: per_device(): normed = lax.all_gather(normed_sub, ('dp', 'vocab'), axis=0, tiled=True)]
    dot_general x6 -> x2, matrix products: 84 us -> 14.7 us  [the longest x1 14.3 us: per_device(): jnp.dot(received.reshape(device_count * sub_rows, half_width), expert_wei...]
    psum x1 -> x0, blocking collectives: 40.6 us -> none  [per_device(): sum_total, target_logit = lax.psum((rescaled, picked_all), ('dp', 'vocab'))]
    pmax x1 -> x0, blocking collectives: 38.6 us -> none  [per_device(): global_peak = lax.pmax(peak_all, ('dp', 'vocab'))]
    unnamed x1 -> x0, blocking collectives: 37.7 us -> none
    all_to_all x1 -> x0, blocking collectives: 27.7 us -> none  [per_device(): lax.all_to_all(buffer, ('dp', 'vocab'), split_axis=0, concat_axis=0, tile...]
  transfers between devices with their start and end apart: 3 -> 0, of which waited for: 2 -> 0; matrix products, arithmetic and copies ran while one was open for 0% -> 0% of each run, Pallas kernels for 0% -> 0%
where the time goes in v1:
time: 297 us
  Pallas kernels  270 us (91%)
  matrix products  14.7 us (5%)
  local copies, waits for them, and re-layouts  10.7 us (4%)
    pallas_call x1, Pallas kernels, head(): pl.pallas_call(functools.partial(head_kernel, bit_count, vocab_count, ord...  128 us
    pallas_call x1, Pallas kernels, combine(): pl.pallas_call(functools.partial(combine_kernel, bit_count, vocab_count,...  99.6 us
    pallas_call x2, Pallas kernels, exchange(): pl.pallas_call(functools.partial(exchange_kernel, count, vocab_count, kin...  42.8 us
    dot_general x1, matrix products, per_device(): jnp.dot(received.reshape(device_count * sub_rows, half_width), expert_wei...  14.3 us

profile of v1, /device:TPU:0, one launch (start us, length us, event | category | flops | bytes accessed | tf_op | source)
XLA Modules:
  0.0 297.0 jit_solution(17149782514476552600)
XLA Ops:
  0.6 0.0 copy-start
  0.7 0.9 constant_dynamic-slice_fusion.2
  1.6 0.1 copy.16
  1.6 0.1 eq.40
  1.7 0.8 constant_dynamic-slice_fusion.1
  2.5 0.1 copy.17
  2.6 0.1 broadcast_in_dim.50
  2.8 0.0 copy-done
  2.8 0.4 convolution_convert_fusion.1
  3.2 0.8 reshape.111
  4.0 0.2 copy.18
  4.3 0.7 dynamic_slice.18
  5.0 27.7 %shard_map.121 = (bf16[32,32,512]{2,1,0:T(8,128)(2,1)S(1)}, s32[32,8,128]{2,1,0:T(8,128)S(1)}) custom-call(bf16[32,32,512]{2,1,0:T(8,128)(2,1)S(1)} %bitcast.24, s32[8,128]{1,0:T(8,128)S(1)} %broadcast_in_dim.55.refs_1_), custom_call_target="tpu_custom_call" | custom-call | tf_op jit(solution)/shard_map/pallas_call | solution.py:95
  32.7 14.3 %convolution_convert_fusion = bf16[1024,7168]{1,0:T(8,128)(2,1)} fusion(bf16[1024,512]{1,0:T(8,128)(2,1)S(1)} %bitcast.26, bf16[1,512,7168]{2,1,0:T(8,128)(2,1)} %param.14), kind=kOutput, calls=%fused_computation | convolution fusion | flops 7523532800 | bytes 23068672 | tf_op jit(solution)/shard_map/dot_general | solution.py:576
  47.0 1.8 constant_dynamic-slice_fusion.token_ref
  48.8 99.6 %shard_map.122 = (bf16[32,7168]{1,0:T(8,128)(2,1)}, bf16[32,7168]{1,0:T(8,128)(2,1)}) custom-call(bf16[2,2,2,2,2,32,7168]{6,5,4,3,2,1,0:T(8,128)(2,1)} %bitcast.27, bf16[32,7168]{1,0:T(8,128)(2,1)} %constant_dynamic-slice_fusion.token_ref, f32[1,7168]{1,0:T(1,128)} %bitcast.35), custom_call_target="tpu_custom_call" | custom-call | tf_op jit(solution)/shard_map/pallas_call | solution.py:470
  148.4 1.1 copy.19.label_ref
  149.5 0.0 copy-start.2
  149.5 0.0 copy-start.3
  149.5 0.0 copy-start.1
  149.5 127.6 %shard_map.123 = (f32[32,32,128]{2,1,0:T(8,128)}, bf16[4,32,7168]{2,1,0:T(8,128)(2,1)}) custom-call(bf16[32,7168]{1,0:T(8,128)(2,1)} %get-tuple-element.10.normed_ref, bf16[32,7168]{1,0:T(8,128)(2,1)} %get-tuple-element.11.layer_ref, s32[32,32,1]{2,1,0:T(8,128)} %copy.19.label_ref, bf16[7168,3584]{1,0:T(8,128)(2,1)} %head_ref.1), custom_call_target="tpu_custom_call" | custom-call | tf_op jit(solution)/shard_map/pallas_call | solution.py:495
  277.1 1.2 copy.21
  278.3 15.2 %shard_map.124 = f32[32,8,128]{2,1,0:T(8,128)S(1)} custom-call(f32[8,8,128]{2,1,0:T(8,128)S(1)} %bitcast.25), custom_call_target="tpu_custom_call" | custom-call | tf_op jit(solution)/shard_map/pallas_call | solution.py:95
  293.5 0.1 fusion.6
  293.6 0.0 copy-done.2
  293.6 0.0 copy-done.3
  293.6 0.5 fusion.5
  294.2 2.8 copy.27
  297.0 0.0 copy-done.1
  (9 shorter events, 0.1 us)
Async XLA Ops:
  0.6 2.1 copy-start
  149.5 144.1 %copy-start.2 = (f32[128]{0:T(128)S(1)}, f32[128]{0:T(128)}, u32[]{:S(2)}) copy-start(f32[128]{0:T(128)} %param.19) | copy-start | bytes 1540
  149.5 144.1 %copy-start.3 = (f32[128]{0:T(128)S(1)}, f32[128]{0:T(128)}, u32[]{:S(2)}) copy-start(f32[128]{0:T(128)} %param.18) | copy-start | bytes 1540
  149.5 147.5 %copy-start.1 = (bf16[128,8,1024]{2,1,0:T(8,128)(2,1)S(1)}, bf16[128,8,1024]{2,1,0:T(8,128)(2,1)}, u32[]{:S(2)}) copy-start(bf16[128,8,1024]{2,1,0:T(8,128)(2,1)} %param.11) | copy-start | bytes 6291460
